TPU v7x, 128 devices: a whole 4x4x4 slice. The times are simulated.
128 devices in a mesh: row: 8 (over z, y_hi), col: 4 (over y_lo, core), feat: 4 (over x).
Axes of the slice: x: 4, y: 4 (y_hi: 2, y_lo: 2; y = y_hi * 2 + y_lo), z: 4, core: 2. Of those that a mesh axis runs over, the one named last changes fastest.
Arguments:
- features: bfloat16 [262144, 128], P(('row', 'col'), 'feat'), may hold values from -6 to 6
- tiles: bfloat16 [8, 4, 1536, 128, 128], P('row', 'col', 'feat'), may hold values from 0 to 0.04321289
- tile_row: int32 [8, 4, 1536], P('row', 'col', 'feat'), may hold values from 0 to 255
- tile_col: int32 [8, 4, 1536], P('row', 'col', 'feat'), may hold values from 0 to 511
- tile_count: int32 [8, 4, 4], P('row', 'col', 'feat'), may hold values from 1 to 384, as said below
- weight: bfloat16 [128, 256], replicated, may hold values from -0.5 to 0.5
- bias: float32 [256], replicated, may hold values from -3 to 3
Outputs:
- output: bfloat16 [262144, 256], P(('row', 'col', 'feat'))
Inputs may be any that keep to these rules, and one draw needn't show every extreme that they name: `tile_count`: some device has all 384 slots live.
All inputs are finite; a program needn't handle non-finite values.
Results may differ from a plain program's by a relative error of at most 0.02.
Values may be sent and summed in bfloat16 or wider, within the bound.
No kernel may reach another device: no remote copies, remote signals or barrier semaphores. Data moves between devices by JAX's collectives and lax.ppermute only.
A program may use at most 128 MiB of HBM per device.

v0:
```python
import jax
import jax.numpy as jnp
from jax import lax
from jax.sharding import PartitionSpec as P


def body(features, tiles, tile_row, tile_col, tile_count, weight, bias):
    node_rows = lax.all_to_all(features, "feat", split_axis=0, concat_axis=1, tiled=True)
    sources = lax.all_gather(node_rows, ("row", "feat"), axis=0, tiled=True)
    tile_side = tiles.shape[-1]
    width = sources.shape[1]
    node_dev = features.shape[0] // lax.axis_size("feat")
    block_rows = lax.axis_size("col") * lax.axis_size("feat") * node_dev // tile_side
    src_blocks = sources.reshape(-1, tile_side, width)
    slot_total = tiles.shape[2]
    tile_stack = tiles.reshape(slot_total, tile_side, tile_side)
    row_index = tile_row.reshape(slot_total)
    col_index = tile_col.reshape(slot_total)
    live_count = tile_count.reshape(())
    block = min(32, slot_total)
    turns = (live_count + block - 1) // block

    def one_turn(turn, partial_value):
        start = turn * block
        tile_block = lax.dynamic_slice_in_dim(tile_stack, start, block, 0)
        rows_here = lax.dynamic_slice_in_dim(row_index, start, block, 0)
        cols_here = lax.dynamic_slice_in_dim(col_index, start, block, 0)
        picked = jnp.take(src_blocks, cols_here, axis=0)
        prods = jnp.einsum("tij,tjf->tif", tile_block, picked, preferred_element_type=jnp.float32)
        live = start + jnp.arange(block, dtype=jnp.int32) < live_count
        prods = jnp.where(live[:, None, None], prods, jnp.zeros_like(prods))
        return partial_value.at[rows_here].add(prods)

    empty = jnp.zeros((block_rows, tile_side, width), jnp.float32)
    partial_value = lax.fori_loop(0, turns, one_turn, empty)
    rounded = lax.optimization_barrier(
        partial_value.reshape(block_rows * tile_side, width).astype(jnp.bfloat16)
    )
    terms = rounded.astype(jnp.float32)
    agg = lax.psum_scatter(
        terms.astype(jnp.bfloat16), ("col", "feat"), scatter_dimension=0, tiled=True
    )
    hidden = jnp.dot(agg, weight, preferred_element_type=jnp.float32) + bias
    return jax.nn.relu(hidden).astype(jnp.bfloat16)


def solution(mesh):
    placed = (
        P(("row", "col"), "feat"),
        P("row", "col", "feat", None, None),
        P("row", "col", "feat"),
        P("row", "col", "feat"),
        P("row", "col", "feat"),
        P(),
        P(),
    )
    return jax.shard_map(
        body, mesh=mesh, in_specs=placed, out_specs=P(("row", "col", "feat"), None), check_vma=False
    )
```

profile of v0, /device:TPU:1, one launch (start us, length us, event | category | flops | bytes accessed | tf_op | source)
XLA Modules:
  0.0 501.4 jit_solution(782019901176667349)
XLA Ops:
  6.5 1.1 copy.17
  7.7 13.3 %all_to_all.19 = bf16[4,2048,32]{1,2,0:T(8,128)(2,1)} all-to-all(bf16[4,2048,32]{1,2,0:T(8,128)(2,1)S(1)} %bitcast.18), channel_id=1, replica_groups=mesh['row'=8,'col'=4,'feat'=4] {'feat'}, dimensions={0} | all-to-all | bytes 1048576 | tf_op jit(solution)/shard_map/all_to_all | solution.py:8
  23.1 150.9 %all-gather.2.cloned.1.call-done = bf16[65536,128]{0,1:T(8,128)(2,1)} async-done(((bf16[2048,128]{0,1:T(8,128)(2,1)}), bf16[65536,128]{0,1:T(8,128)(2,1)}) %all-gather.2.cloned.1.call-update) | async-done | bytes 16777232 | tf_op jit(solution)/shard_map/all_gather | solution.py:9
  174.0 22.4 %copy.14 = bf16[65536,128]{1,0:T(8,128)(2,1)} copy(bf16[65536,128]{0,1:T(8,128)(2,1)} %all-gather.2.cloned.1.call-done) | data formatting | bytes 33554432 | tf_op jit(solution)/shard_map/while | solution.py:35
  196.4 7.8 %broadcast_in_dim.28 = f32[256,128,128]{2,1,0:T(8,128)} broadcast(f32[]{:T(128)} %constant.47.clone.1), dimensions={} | broadcast | bytes 16777220 | tf_op jit(solution)/shard_map/broadcast_in_dim | solution.py:34
  204.3 106.8 %while.10 = (s32[]{:T(128)}, f32[256,128,128]{2,1,0:T(8,128)}, s32[]{:T(128)}, s32[384]{0:T(512)S(1)}, s32[]{:T(128)}, /*index=5*/bf16[384,128,128]{2,1,0:T(8,12...) while((s32[]{:T(128)}, f32[256,128,128]{2,1,0:T(8,128)}, ...), condition=%wide.region_2.3_spmd, body=%wide.region_0.2_spmd.sunk | while | flops 135791968 | bytes 12588215 | solution.py:35
  205.1 6.5 %gather_fusion = bf16[32,128,128]{2,1,0:T(8,128)(2,1)S(1)} fusion(bf16[512,128,128]{2,1,0:T(8,128)(2,1)} %get-tuple-element.179, s32[1024]{0:T(1024)S(1)} %pad_clamp_fusion.2), kind=kCustom, calls=%fused_computation.clone.1 | custom fusion | bytes 2097280 | tf_op jit(solution)/shard_map/while/body/jit(_take)/gather | solution.py:28
  211.6 1.7 convolution_select_fusion.2
  213.4 6.2 %scatter_fusion = f32[256,128,128]{2,1,0:T(8,128)} fusion(f32[256,128,128]{2,1,0:T(8,128)} %get-tuple-element.161, s32[32]{0:T(128)S(1)} %compare_select_fusion.4, f32[32,128,128]{2,1,0:T(8,128)S(1)} %convolution_select_fusion.2), kind=kCustom, calls=%fused_computation.1.clone.1 | custom fusion | flops 524288 | bytes 6291584 | tf_op jit(solution)/shard_map/while/body/scatter-add | solution.py:32
  219.7 0.7 compare_and_fusion.2
  220.4 6.5 %gather_fusion = bf16[32,128,128]{2,1,0:T(8,128)(2,1)S(1)} fusion(bf16[512,128,128]{2,1,0:T(8,128)(2,1)} %get-tuple-element.179, s32[1024]{0:T(1024)S(1)} %pad_clamp_fusion.2), kind=kCustom, calls=%fused_computation.clone.1 | custom fusion | bytes 2097280 | tf_op jit(solution)/shard_map/while/body/jit(_take)/gather | solution.py:28
  226.9 1.7 convolution_select_fusion.2
  228.7 6.2 %scatter_fusion = f32[256,128,128]{2,1,0:T(8,128)} fusion(f32[256,128,128]{2,1,0:T(8,128)} %get-tuple-element.161, s32[32]{0:T(128)S(1)} %compare_select_fusion.4, f32[32,128,128]{2,1,0:T(8,128)S(1)} %convolution_select_fusion.2), kind=kCustom, calls=%fused_computation.1.clone.1 | custom fusion | flops 524288 | bytes 6291584 | tf_op jit(solution)/shard_map/while/body/scatter-add | solution.py:32
  235.7 6.5 %gather_fusion = bf16[32,128,128]{2,1,0:T(8,128)(2,1)S(1)} fusion(bf16[512,128,128]{2,1,0:T(8,128)(2,1)} %get-tuple-element.179, s32[1024]{0:T(1024)S(1)} %pad_clamp_fusion.2), kind=kCustom, calls=%fused_computation.clone.1 | custom fusion | bytes 2097280 | tf_op jit(solution)/shard_map/while/body/jit(_take)/gather | solution.py:28
  242.2 1.7 convolution_select_fusion.2
  244.0 6.1 %scatter_fusion = f32[256,128,128]{2,1,0:T(8,128)} fusion(f32[256,128,128]{2,1,0:T(8,128)} %get-tuple-element.161, s32[32]{0:T(128)S(1)} %compare_select_fusion.4, f32[32,128,128]{2,1,0:T(8,128)S(1)} %convolution_select_fusion.2), kind=kCustom, calls=%fused_computation.1.clone.1 | custom fusion | flops 524288 | bytes 6291584 | tf_op jit(solution)/shard_map/while/body/scatter-add | solution.py:32
  250.2 0.7 compare_and_fusion.2
  250.9 6.5 %gather_fusion = bf16[32,128,128]{2,1,0:T(8,128)(2,1)S(1)} fusion(bf16[512,128,128]{2,1,0:T(8,128)(2,1)} %get-tuple-element.179, s32[1024]{0:T(1024)S(1)} %pad_clamp_fusion.2), kind=kCustom, calls=%fused_computation.clone.1 | custom fusion | bytes 2097280 | tf_op jit(solution)/shard_map/while/body/jit(_take)/gather | solution.py:28
  257.4 1.7 convolution_select_fusion.2
  259.2 6.2 %scatter_fusion = f32[256,128,128]{2,1,0:T(8,128)} fusion(f32[256,128,128]{2,1,0:T(8,128)} %get-tuple-element.161, s32[32]{0:T(128)S(1)} %compare_select_fusion.4, f32[32,128,128]{2,1,0:T(8,128)S(1)} %convolution_select_fusion.2), kind=kCustom, calls=%fused_computation.1.clone.1 | custom fusion | flops 524288 | bytes 6291584 | tf_op jit(solution)/shard_map/while/body/scatter-add | solution.py:32
  266.2 6.5 %gather_fusion = bf16[32,128,128]{2,1,0:T(8,128)(2,1)S(1)} fusion(bf16[512,128,128]{2,1,0:T(8,128)(2,1)} %get-tuple-element.179, s32[1024]{0:T(1024)S(1)} %pad_clamp_fusion.2), kind=kCustom, calls=%fused_computation.clone.1 | custom fusion | bytes 2097280 | tf_op jit(solution)/shard_map/while/body/jit(_take)/gather | solution.py:28
  272.8 1.7 convolution_select_fusion.2
  274.5 6.2 %scatter_fusion = f32[256,128,128]{2,1,0:T(8,128)} fusion(f32[256,128,128]{2,1,0:T(8,128)} %get-tuple-element.161, s32[32]{0:T(128)S(1)} %compare_select_fusion.4, f32[32,128,128]{2,1,0:T(8,128)S(1)} %convolution_select_fusion.2), kind=kCustom, calls=%fused_computation.1.clone.1 | custom fusion | flops 524288 | bytes 6291584 | tf_op jit(solution)/shard_map/while/body/scatter-add | solution.py:32
  281.5 6.5 %gather_fusion = bf16[32,128,128]{2,1,0:T(8,128)(2,1)S(1)} fusion(bf16[512,128,128]{2,1,0:T(8,128)(2,1)} %get-tuple-element.179, s32[1024]{0:T(1024)S(1)} %pad_clamp_fusion.2), kind=kCustom, calls=%fused_computation.clone.1 | custom fusion | bytes 2097280 | tf_op jit(solution)/shard_map/while/body/jit(_take)/gather | solution.py:28
  288.0 1.7 convolution_select_fusion.2
  289.8 6.1 %scatter_fusion = f32[256,128,128]{2,1,0:T(8,128)} fusion(f32[256,128,128]{2,1,0:T(8,128)} %get-tuple-element.161, s32[32]{0:T(128)S(1)} %compare_select_fusion.4, f32[32,128,128]{2,1,0:T(8,128)S(1)} %convolution_select_fusion.2), kind=kCustom, calls=%fused_computation.1.clone.1 | custom fusion | flops 524288 | bytes 6291584 | tf_op jit(solution)/shard_map/while/body/scatter-add | solution.py:32
  296.7 6.5 %gather_fusion = bf16[32,128,128]{2,1,0:T(8,128)(2,1)S(1)} fusion(bf16[512,128,128]{2,1,0:T(8,128)(2,1)} %get-tuple-element.179, s32[1024]{0:T(1024)S(1)} %pad_clamp_fusion.2), kind=kCustom, calls=%fused_computation.clone.1 | custom fusion | bytes 2097280 | tf_op jit(solution)/shard_map/while/body/jit(_take)/gather | solution.py:28
  303.2 1.7 convolution_select_fusion.2
  305.0 6.1 %scatter_fusion = f32[256,128,128]{2,1,0:T(8,128)} fusion(f32[256,128,128]{2,1,0:T(8,128)} %get-tuple-element.161, s32[32]{0:T(128)S(1)} %compare_select_fusion.4, f32[32,128,128]{2,1,0:T(8,128)S(1)} %convolution_select_fusion.2), kind=kCustom, calls=%fused_computation.1.clone.1 | custom fusion | flops 524288 | bytes 6291584 | tf_op jit(solution)/shard_map/while/body/scatter-add | solution.py:32
  311.1 9.2 %convert_element_type.11 = bf16[256,128,128]{2,1,0:T(8,128)(2,1)} convert(f32[256,128,128]{2,1,0:T(8,128)} %get-tuple-element.48) | non-fusion elementwise | flops 4194304 | bytes 25165824 | tf_op jit(solution)/shard_map/convert_element_type | solution.py:37
  320.3 171.8 %reduce-scatter.2.cloned.1.call-done = bf16[2048,128]{1,0:T(8,128)(2,1)} async-done(((bf16[32768,128]{1,0:T(8,128)(2,1)}), bf16[2048,128]{1,0:T(8,128)(2,1)}) %reduce-scatter.2.cloned.1.call-update) | async-done | bytes 524304 | tf_op jit(solution)/shard_map/reduce_scatter | solution.py:40
  492.2 2.4 fusion.7
  (29 shorter events, 5.7 us)
Async XLA Ops:
  6.5 485.6 %copy-start = (bf16[128,256]{1,0:T(8,128)(2,1)S(1)}, bf16[128,256]{1,0:T(8,128)(2,1)}, u32[]{:S(2)}) copy-start(bf16[128,256]{1,0:T(8,128)(2,1)} %param.14) | copy-start | bytes 196612
  6.5 167.5 %all-gather.2.cloned.1.call-start = ((), (), s32[]{:S(2)}) async-start(), calls=%async_computation.2 | async-start | bytes 17301504 | tf_op jit(solution)/shard_map/all_gather | solution.py:9
  21.0 471.2 %reduce-scatter.2.cloned.1.call-start = ((), (), s32[]{:S(2)}) async-start(), calls=%async_computation.3 | async-start | bytes 8912896 | tf_op jit(solution)/shard_map/reduce_scatter | solution.py:40
  311.1 181.1 %copy-start.1 = (f32[256]{0:T(256)S(1)}, f32[256]{0:T(256)}, u32[]{:S(2)}) copy-start(f32[256]{0:T(256)} %param.15) | copy-start | bytes 3076
Sparse Core Ops, SparseCore 0:
  21.1 152.8 all-gather.1
  320.5 171.6 reduce-scatter.1
where the time goes:
time: 505 us; the launch traced here: 501 us
  waiting for transfers between devices  323 us (64%)
  local copies, waits for them, and re-layouts  77 us (15%)
  other arithmetic  59.5 us (12%)
  matrix products  14.6 us (3%)
  between operations  14.1 us (3%)
  blocking collectives  13.3 us (3%)
    reduce_scatter x1, waiting for transfers between devices, body(): lax.psum_scatter(terms.astype(jnp.bfloat16), ('col', 'feat'), scatter_dim...  172 us
    all_gather x1, waiting for transfers between devices, body(): sources = lax.all_gather(node_rows, ('row', 'feat'), axis=0, tiled=True)  151 us
    gather x7, local copies, waits for them, and re-layouts, one_turn(): picked = jnp.take(src_blocks, cols_here, axis=0)  45.6 us
    scatter-add x7, other arithmetic, one_turn(): return partial_value.at[rows_here].add(prods)  43.3 us
    while x1, local copies, waits for them, and re-layouts, body(): partial_value = lax.fori_loop(0, turns, one_turn, empty)  22.4 us
    all_to_all x1, blocking collectives, body(): lax.all_to_all(features, 'feat', split_axis=0, concat_axis=1, tiled=True)  13.3 us
    dot_general x7, matrix products, one_turn(): jnp.einsum('tij,tjf->tif', tile_block, picked, preferred_element_type=jnp...  12.2 us
  transfers between devices with their start and end apart: 2, of which 2 were waited for; matrix products, arithmetic and copies ran while one was open for 0% of the time, Pallas kernels for 0%

commit v1 on v0

--- a/solution.py
+++ b/solution.py
@@ -6,7 +6,10 @@
 
 def body(features, tiles, tile_row, tile_col, tile_count, weight, bias):
     node_rows = lax.all_to_all(features, "feat", split_axis=0, concat_axis=1, tiled=True)
-    sources = lax.all_gather(node_rows, ("row", "feat"), axis=0, tiled=True)
+    devices = lax.axis_size(("row", "feat"))
+    blocks = jnp.stack([node_rows for _ in range(devices)])
+    blocks = lax.all_to_all(blocks, ("row", "feat"), split_axis=0, concat_axis=0)
+    sources = jnp.concatenate(blocks, axis=0)
     tile_side = tiles.shape[-1]
     width = sources.shape[1]
     node_dev = features.shape[0] // lax.axis_size("feat")

time: 505 us -> 623 us (1.23)
  waiting for transfers between devices: 323 us -> 450 us
  local copies, waits for them, and re-layouts: 77 us -> 61.1 us
  starting transfers between devices: 0.04 us -> 8.96 us
    all_to_all x0 -> x1, waiting for transfers between devices: none -> 256 us  [body(): lax.all_to_all(blocks, ('row', 'feat'), split_axis=0, concat_axis=0)]
    all_gather x1 -> x0, waiting for transfers between devices: 151 us -> none  [body(): sources = lax.all_gather(node_rows, ('row', 'feat'), axis=0, tiled=True)]
    while x1 -> x0, local copies, waits for them, and re-layouts: 22.4 us -> none  [body(): partial_value = lax.fori_loop(0, turns, one_turn, empty)]
    reduce_scatter x1, waiting for transfers between devices: 172 us -> 193 us  [body(): lax.psum_scatter(terms.astype(jnp.bfloat16), ('col', 'feat'), scatter_dim...]
    all_to_all x0 -> x1, starting transfers between devices: none -> 8.92 us  [body(): lax.all_to_all(blocks, ('row', 'feat'), split_axis=0, concat_axis=0)]
    another operation x0 -> x2, local copies, waits for them, and re-layouts: none -> 6.48 us  [body(): blocks = jnp.stack([node_rows for _ in range(devices)])]
where the time goes in v1:
time: 623 us; the launch traced here: 620 us
  waiting for transfers between devices  450 us (72%)
  local copies, waits for them, and re-layouts  61.1 us (10%)
  other arithmetic  58.1 us (9%)
  matrix products  14.6 us (2%)
  between operations  14.1 us (2%)
  blocking collectives  13.2 us (2%)
  starting transfers between devices  8.96 us (1%)
    all_to_all x1, waiting for transfers between devices, body(): lax.all_to_all(blocks, ('row', 'feat'), split_axis=0, concat_axis=0)  256 us
    reduce_scatter x1, waiting for transfers between devices, body(): lax.psum_scatter(terms.astype(jnp.bfloat16), ('col', 'feat'), scatter_dim...  193 us
    gather x7, local copies, waits for them, and re-layouts, one_turn(): picked = jnp.take(src_blocks, cols_here, axis=0)  45.6 us
    scatter-add x7, other arithmetic, one_turn(): return partial_value.at[rows_here].add(prods)  43.3 us
    all_to_all x1, blocking collectives, body(): lax.all_to_all(features, 'feat', split_axis=0, concat_axis=1, tiled=True)  13.2 us
  transfers between devices with their start and end apart: 2, of which 2 were waited for; matrix products, arithmetic and copies ran while one was open for 0% of the time, Pallas kernels for 0%

profile of v1, /device:TPU:1, one launch (start us, length us, event | category | flops | bytes accessed | tf_op | source)
XLA Modules:
  0.0 619.8 jit_solution(4039854854583370831)
XLA Ops:
  6.5 1.1 copy.15
  7.6 13.2 %all_to_all.21 = bf16[4,2048,32]{1,2,0:T(8,128)(2,1)S(1)} all-to-all(bf16[4,2048,32]{1,2,0:T(8,128)(2,1)S(1)} %bitcast.17), channel_id=1, replica_groups=mesh['row'=8,'col'=4,'feat'=4] {'feat'}, dimensions={0} | all-to-all | bytes 1048576 | tf_op jit(solution)/shard_map/all_to_all | solution.py:8
  21.1 6.2 %stack.5 = bf16[32,2048,128]{2,1,0:T(8,128)(2,1)} broadcast(bf16[2048,128]{1,0:T(8,128)(2,1)S(1)} %copy.12), dimensions={1,2} | broadcast | bytes 17301504 | tf_op jit(solution)/shard_map/stack | solution.py:10
  27.3 8.9 %all-to-all-start.1 = ((bf16[32,2048,128]{2,1,0:T(8,128)(2,1)}), bf16[32,2048,128]{2,1,0:T(8,128)(2,1)}, u32[]{:S(2)}, u32[]{:S(2)}) async-start(bf16[32,2048,128]{2,1,0:T(8,128)(2,1)} %stack.5), calls=%async_computation.1 | async-start | bytes 33554432 | tf_op jit(solution)/shard_map/all_to_all | solution.py:11
  37.1 256.2 %all-to-all-done.1 = bf16[32,2048,128]{2,1,0:T(8,128)(2,1)} async-done(((bf16[32,2048,128]{2,1,0:T(8,128)(2,1)}), bf16[32,2048,128]{2,1,0:T(8,128)(2,1)}, u32[]{:S(2)}, u32[]{:S(2)}) %all-to-all-start.1) | async-done | bytes 16777248 | tf_op jit(solution)/shard_map/all_to_all | solution.py:11
  293.2 7.8 %broadcast_in_dim.28 = f32[256,128,128]{2,1,0:T(8,128)} broadcast(f32[]{:T(128)} %constant.47.clone.1), dimensions={} | broadcast | bytes 16777220 | tf_op jit(solution)/shard_map/broadcast_in_dim | solution.py:37
  301.1 106.8 %while.10 = (s32[]{:T(128)}, f32[256,128,128]{2,1,0:T(8,128)}, s32[]{:T(128)}, s32[384]{0:T(512)S(1)}, s32[]{:T(128)}, /*index=5*/bf16[384,128,128]{2,1,0:T(8,12...) while((s32[]{:T(128)}, f32[256,128,128]{2,1,0:T(8,128)}, ...), condition=%wide.region_2.3_spmd, body=%wide.region_0.2_spmd.sunk | while | flops 135791968 | bytes 12588215 | solution.py:38
  301.1 0.7 compare_and_fusion.2
  301.9 6.5 %gather_fusion = bf16[32,128,128]{2,1,0:T(8,128)(2,1)S(1)} fusion(bf16[512,128,128]{2,1,0:T(8,128)(2,1)} %get-tuple-element.155, s32[1024]{0:T(1024)S(1)} %pad_clamp_fusion.2), kind=kCustom, calls=%fused_computation.clone.1 | custom fusion | bytes 2097280 | tf_op jit(solution)/shard_map/while/body/jit(_take)/gather | solution.py:31
  308.4 1.7 convolution_select_fusion.2
  310.1 6.2 %scatter_fusion = f32[256,128,128]{2,1,0:T(8,128)} fusion(f32[256,128,128]{2,1,0:T(8,128)} %get-tuple-element.137, s32[32]{0:T(128)S(1)} %compare_select_fusion.4, f32[32,128,128]{2,1,0:T(8,128)S(1)} %convolution_select_fusion.2), kind=kCustom, calls=%fused_computation.1.clone.1 | custom fusion | flops 524288 | bytes 6291584 | tf_op jit(solution)/shard_map/while/body/scatter-add | solution.py:35
  317.2 6.5 %gather_fusion = bf16[32,128,128]{2,1,0:T(8,128)(2,1)S(1)} fusion(bf16[512,128,128]{2,1,0:T(8,128)(2,1)} %get-tuple-element.155, s32[1024]{0:T(1024)S(1)} %pad_clamp_fusion.2), kind=kCustom, calls=%fused_computation.clone.1 | custom fusion | bytes 2097280 | tf_op jit(solution)/shard_map/while/body/jit(_take)/gather | solution.py:31
  323.7 1.7 convolution_select_fusion.2
  325.5 6.2 %scatter_fusion = f32[256,128,128]{2,1,0:T(8,128)} fusion(f32[256,128,128]{2,1,0:T(8,128)} %get-tuple-element.137, s32[32]{0:T(128)S(1)} %compare_select_fusion.4, f32[32,128,128]{2,1,0:T(8,128)S(1)} %convolution_select_fusion.2), kind=kCustom, calls=%fused_computation.1.clone.1 | custom fusion | flops 524288 | bytes 6291584 | tf_op jit(solution)/shard_map/while/body/scatter-add | solution.py:35
  332.5 6.5 %gather_fusion = bf16[32,128,128]{2,1,0:T(8,128)(2,1)S(1)} fusion(bf16[512,128,128]{2,1,0:T(8,128)(2,1)} %get-tuple-element.155, s32[1024]{0:T(1024)S(1)} %pad_clamp_fusion.2), kind=kCustom, calls=%fused_computation.clone.1 | custom fusion | bytes 2097280 | tf_op jit(solution)/shard_map/while/body/jit(_take)/gather | solution.py:31
  339.0 1.7 convolution_select_fusion.2
  340.7 6.1 scatter_fusion
  347.7 6.5 %gather_fusion = bf16[32,128,128]{2,1,0:T(8,128)(2,1)S(1)} fusion(bf16[512,128,128]{2,1,0:T(8,128)(2,1)} %get-tuple-element.155, s32[1024]{0:T(1024)S(1)} %pad_clamp_fusion.2), kind=kCustom, calls=%fused_computation.clone.1 | custom fusion | bytes 2097280 | tf_op jit(solution)/shard_map/while/body/jit(_take)/gather | solution.py:31
  354.2 1.7 convolution_select_fusion.2
  355.9 6.2 %scatter_fusion = f32[256,128,128]{2,1,0:T(8,128)} fusion(f32[256,128,128]{2,1,0:T(8,128)} %get-tuple-element.137, s32[32]{0:T(128)S(1)} %compare_select_fusion.4, f32[32,128,128]{2,1,0:T(8,128)S(1)} %convolution_select_fusion.2), kind=kCustom, calls=%fused_computation.1.clone.1 | custom fusion | flops 524288 | bytes 6291584 | tf_op jit(solution)/shard_map/while/body/scatter-add | solution.py:35
  363.0 6.5 %gather_fusion = bf16[32,128,128]{2,1,0:T(8,128)(2,1)S(1)} fusion(bf16[512,128,128]{2,1,0:T(8,128)(2,1)} %get-tuple-element.155, s32[1024]{0:T(1024)S(1)} %pad_clamp_fusion.2), kind=kCustom, calls=%fused_computation.clone.1 | custom fusion | bytes 2097280 | tf_op jit(solution)/shard_map/while/body/jit(_take)/gather | solution.py:31
  369.5 1.7 convolution_select_fusion.2
  371.3 6.2 scatter_fusion
  378.3 6.5 %gather_fusion = bf16[32,128,128]{2,1,0:T(8,128)(2,1)S(1)} fusion(bf16[512,128,128]{2,1,0:T(8,128)(2,1)} %get-tuple-element.155, s32[1024]{0:T(1024)S(1)} %pad_clamp_fusion.2), kind=kCustom, calls=%fused_computation.clone.1 | custom fusion | bytes 2097280 | tf_op jit(solution)/shard_map/while/body/jit(_take)/gather | solution.py:31
  384.8 1.7 convolution_select_fusion.2
  386.5 6.1 scatter_fusion
  393.5 6.5 %gather_fusion = bf16[32,128,128]{2,1,0:T(8,128)(2,1)S(1)} fusion(bf16[512,128,128]{2,1,0:T(8,128)(2,1)} %get-tuple-element.155, s32[1024]{0:T(1024)S(1)} %pad_clamp_fusion.2), kind=kCustom, calls=%fused_computation.clone.1 | custom fusion | bytes 2097280 | tf_op jit(solution)/shard_map/while/body/jit(_take)/gather | solution.py:31
  400.0 1.7 convolution_select_fusion.2
  401.7 6.1 scatter_fusion
  407.9 9.2 %convert_element_type.11 = bf16[256,128,128]{2,1,0:T(8,128)(2,1)} convert(f32[256,128,128]{2,1,0:T(8,128)} %get-tuple-element.48) | non-fusion elementwise | flops 4194304 | bytes 25165824 | tf_op jit(solution)/shard_map/convert_element_type | solution.py:40
  417.1 193.4 %reduce-scatter.2.cloned.1.call-done = bf16[2048,128]{1,0:T(8,128)(2,1)} async-done(((bf16[32768,128]{1,0:T(8,128)(2,1)}), bf16[2048,128]{1,0:T(8,128)(2,1)}) %reduce-scatter.2.cloned.1.call-update) | async-done | bytes 524304 | tf_op jit(solution)/shard_map/reduce_scatter | solution.py:43
  610.5 2.4 fusion.7
  (33 shorter events, 5.3 us)
Async XLA Ops:
  6.5 604.0 %copy-start = (bf16[128,256]{1,0:T(8,128)(2,1)S(1)}, bf16[128,256]{1,0:T(8,128)(2,1)}, u32[]{:S(2)}) copy-start(bf16[128,256]{1,0:T(8,128)(2,1)} %param.14) | copy-start | bytes 196612
  27.3 9.6 %copy-start.1 = (s32[1,1,384]{2,1,0:T(1,128)S(1)}, s32[1,1,384]{2,1,0:T(1,128)}, u32[]{:S(2)}) copy-start(s32[1,1,384]{2,1,0:T(1,128)} %param.11) | copy-start | bytes 4612
  27.3 9.7 %copy-start.2 = (s32[1,1,384]{2,1,0:T(1,128)S(1)}, s32[1,1,384]{2,1,0:T(1,128)}, u32[]{:S(2)}) copy-start(s32[1,1,384]{2,1,0:T(1,128)} %param.12) | copy-start | bytes 4612
  27.3 265.9 %all-to-all-start.1 = ((bf16[32,2048,128]{2,1,0:T(8,128)(2,1)}), bf16[32,2048,128]{2,1,0:T(8,128)(2,1)}, u32[]{:S(2)}, u32[]{:S(2)}) async-start(bf16[32,2048,128]{2,1,0:T(8,128)(2,1)} %stack.5), calls=%async_computation.1 | async-start | bytes 33554432 | tf_op jit(solution)/shard_map/all_to_all | solution.py:11
  36.3 574.2 %reduce-scatter.2.cloned.1.call-start = ((), (), s32[]{:S(2)}) async-start(), calls=%async_computation.3 | async-start | bytes 8912896 | tf_op jit(solution)/shard_map/reduce_scatter | solution.py:43
  407.9 202.7 %copy-start.3 = (f32[256]{0:T(256)S(1)}, f32[256]{0:T(256)}, u32[]{:S(2)}) copy-start(f32[256]{0:T(256)} %param.15) | copy-start | bytes 3076
Sparse Core Ops, SparseCore 0:
  417.2 193.2 reduce-scatter.1
